TPU v7x, 32 devices: a whole 2x2x4 slice. The times are simulated.
32 devices in a mesh: seq: 8 (over z, core), head: 4 (over y, x).
Axes of the slice: x: 2, y: 2, z: 4, core: 2. Of those that a mesh axis runs over, the one named last changes fastest.
Arguments:
- tokens: bfloat16 [4096, 2304], P(('seq', 'head')), may hold values from -6 to 6
- in_gain: float32 [2304], replicated, may hold values from 0.5 to 1.5
- out_gain: float32 [2304], replicated, may hold values from 0.5 to 1.5
- query_weight: bfloat16 [2304, 2048], P(None, 'head'), may hold values from -1.25 to 1.25
- keyval_weight: bfloat16 [2304, 2048], replicated, may hold values from -0.125 to 0.125
- out_weight: bfloat16 [2048, 2304], P('head'), may hold values from -0.125 to 0.125
- cache_entries: bfloat16 [4, 2048, 512], P(None, 'seq'), may hold values from -6 to 6
- segment_ids: int32 [4096], P('seq'), may hold values from -1 to 63, as said below
- cache_lengths: int32 [64], replicated, may hold values from 0 to 512, as said below
- block_owners: int32 [128], P('seq'), may hold values from -1 to 63, as said below
Outputs:
- layer_out: bfloat16 [4096, 2304], P(('seq', 'head'))
Inputs may be any that keep to these rules, and one draw needn't show every extreme that they name: `segment_ids`: valid slots come first and their ids never fall; every id from 0 to 63 has at least one slot; padding slots, marked -1, fill the end of the stream; exactly one segment has 2048 slots and none has more. `block_owners`: the segment that owns each cache block, or -1 for a free block; a segment's cache fills its blocks in the order of their indices; no segment owns more than 32 blocks. `cache_lengths`: zero for a segment without blocks, and some segment has none; otherwise more than 16 times one less than its number of blocks and at most 16 times that number; exactly one segment holds 512 rows.
All inputs are finite; a program needn't handle non-finite values.
Results may differ from a plain program's by a relative error of at most 0.012.
Values may be sent and summed in bfloat16 or wider, within the bound.
A program may use at most 128 MiB of HBM per device.

v0:
```python
import math
import jax
import jax.numpy as jnp
from jax import lax
from jax.sharding import PartitionSpec as P

QH = 8
KVH = 4
HD = 256
NSEG = 64
BLK = 16
EPSILON = 1e-06
SOFT_CAP = 50.0


def carried_in(array, axis, combine, identity):
    devices, position = (lax.axis_size(axis), lax.axis_index(axis))
    everything = jax.tree.map(lambda part: lax.all_gather(part, axis), array)
    start = jax.tree.map(
        lambda part, zero: jnp.broadcast_to(jnp.asarray(zero, part.dtype), part.shape),
        array,
        identity,
    )

    def hop(k, before):
        reached = k < position
        new = combine(before, jax.tree.map(lambda part: part[k], everything))
        return jax.tree.map(lambda a, b: jnp.where(reached, a, b), new, before)

    return lax.fori_loop(0, devices, hop, start)


def rms_scale(matrix, scaling):
    matrix = matrix.astype(jnp.float32)
    mean_square = jnp.mean(matrix * matrix, axis=-1, keepdims=True)
    return matrix * lax.rsqrt(mean_square + EPSILON) * scaling


def frequencies(extent):
    return 10000.0 ** (-(jnp.arange(extent // 2, dtype=jnp.float32) * 2.0 / extent))


def rotate(vectors, angles):
    half_width = vectors.shape[-1] // 2
    leading = vectors[..., :half_width]
    trailing = vectors[..., half_width:]
    cosine = jnp.cos(angles)
    sine_part = jnp.sin(angles)
    return jnp.concatenate(
        [leading * cosine - trailing * sine_part, trailing * cosine + leading * sine_part], axis=-1
    )


def attention_fold(queries, q_seg, q_slot, key_width):
    present = q_seg >= 0

    def advance(totals, key_block):
        pair_rows, key_seg, key_slot = key_block
        numerator, denominator = totals
        scores = jnp.einsum(
            "qhd,kd->qhk", queries, pair_rows[:, :key_width], preferred_element_type=jnp.float32
        )
        scores = SOFT_CAP * jnp.tanh(scores / SOFT_CAP)
        allowed = (
            (key_seg[None, :] == q_seg[:, None])
            & (key_slot[None, :] <= q_slot[:, None])
            & present[:, None]
        )
        weights = jnp.where(allowed[:, None, :], jnp.exp(scores), 0.0)
        denominator = denominator + jnp.sum(weights, axis=-1)
        numerator = numerator + jnp.einsum(
            "qhk,kd->qhd",
            weights.astype(jnp.bfloat16),
            pair_rows[:, key_width:],
            preferred_element_type=jnp.float32,
        )
        return ((numerator, denominator), None)

    def folding(totals, portion, offset):
        pair_rows, key_seg, key_slot = portion
        row_count = pair_rows.shape[0]
        block_rows = math.gcd(row_count, 1024)
        block_count = row_count // block_rows
        blocks = (
            pair_rows.reshape(block_count, block_rows, pair_rows.shape[1]),
            key_seg.reshape(block_count, block_rows),
            key_slot.reshape(block_count, block_rows),
        )
        totals, _ = lax.scan(advance, totals, blocks)
        return totals

    return folding


def local(
    tokens,
    in_gain,
    out_gain,
    query_weight,
    keyval_weight,
    out_weight,
    cache_entries,
    segment_ids,
    cache_lengths,
    block_owners,
):
    heads_here = query_weight.shape[1] // HD
    group_size = QH // KVH
    seq_index = lax.axis_index("seq")
    head_index = lax.axis_index("head")
    shared_head = head_index * heads_here // group_size
    stream_rows = segment_ids.shape[0]
    seg_range = jnp.arange(NSEG, dtype=jnp.int32)
    matches = (segment_ids[:, None] == seg_range[None, :]).astype(jnp.int32)
    counts = jnp.sum(matches, axis=0)
    owner_match = (block_owners[:, None] == seg_range[None, :]).astype(jnp.int32)
    owned_count = jnp.sum(owner_match, axis=0)

    def add_pairs(earlier, later):
        return (earlier[0] + later[0], earlier[1] + later[1])

    empty_counts = jnp.zeros((NSEG,), jnp.int32)
    before_tokens, before_blocks = carried_in(
        (counts, owned_count), "seq", add_pairs, (empty_counts, empty_counts)
    )
    first_local = jnp.cumsum(counts) - counts
    local_slot = jnp.arange(stream_rows, dtype=jnp.int32)
    positions = (
        jnp.sum(matches * (cache_lengths + before_tokens - first_local)[None, :], axis=1)
        + local_slot
    )
    q_slot = seq_index * stream_rows + local_slot
    angles_all = positions.astype(jnp.float32)[:, None] * frequencies(HD)[None, :]
    block_rank = jnp.sum(
        owner_match * (jnp.cumsum(owner_match, axis=0) - owner_match + before_blocks[None, :]),
        axis=1,
    )
    limits = jnp.sum(owner_match * cache_lengths[None, :], axis=1)
    offsets = jnp.arange(BLK, dtype=jnp.int32)
    usable = (block_owners[:, None] >= 0) & (
        block_rank[:, None] * BLK + offsets[None, :] < limits[:, None]
    )
    cache_seg = jnp.where(usable, block_owners[:, None], -1).reshape(-1)
    cache_pairs = lax.dynamic_index_in_dim(cache_entries, shared_head, 0, keepdims=False)
    cache_slot = jnp.full((cache_seg.shape[0],), -1, jnp.int32)
    w_shared = lax.dynamic_slice_in_dim(keyval_weight, shared_head * 2 * HD, 2 * HD, 1)
    portion = lax.all_gather(tokens, "head", axis=0, tiled=True)
    row_count = portion.shape[0]
    normed = rms_scale(portion, in_gain).astype(jnp.bfloat16)
    query_rows = jnp.dot(normed, query_weight, preferred_element_type=jnp.float32).reshape(
        row_count, heads_here, HD
    )
    query_rows = (rotate(query_rows, angles_all[:, None, :]) * HD ** (-0.5)).astype(jnp.bfloat16)
    keyval = jnp.dot(normed, w_shared, preferred_element_type=jnp.float32)
    key_rows = rotate(keyval[:, :HD], angles_all).astype(jnp.bfloat16)
    value_rows = keyval[:, HD:].astype(jnp.bfloat16)
    projected = jnp.concatenate(
        [query_rows.reshape(row_count, heads_here * HD), key_rows, value_rows], axis=1
    )
    queries = projected[:, : heads_here * HD].reshape(stream_rows, heads_here, HD)
    new_pairs = projected[:, heads_here * HD :]
    folding = attention_fold(queries, segment_ids, q_slot, HD)
    start_totals = (
        jnp.zeros((stream_rows, heads_here, HD), jnp.float32),
        jnp.zeros((stream_rows, heads_here), jnp.float32),
    )
    partial_value = folding(
        start_totals,
        (
            lax.all_gather(new_pairs, "seq", axis=0, tiled=True),
            lax.all_gather(segment_ids, "seq", axis=0, tiled=True),
            lax.all_gather(q_slot, "seq", axis=0, tiled=True),
        ),
        jnp.int32(0),
    )
    numerator, denominator = folding(
        partial_value,
        (
            lax.all_gather(cache_pairs, "seq", axis=0, tiled=True),
            lax.all_gather(cache_seg, "seq", axis=0, tiled=True),
            lax.all_gather(cache_slot, "seq", axis=0, tiled=True),
        ),
        jnp.int32(0),
    )
    present = segment_ids >= 0
    safe = jnp.where(present[:, None], denominator, 1.0)
    attended = jnp.where(present[:, None, None], numerator / safe[:, :, None], 0.0)
    attended = attended.astype(jnp.bfloat16).reshape(stream_rows, heads_here * HD)
    branch = lax.psum_scatter(
        jnp.dot(attended, out_weight, preferred_element_type=jnp.float32),
        "head",
        scatter_dimension=0,
        tiled=True,
    )
    return (tokens.astype(jnp.float32) + rms_scale(branch, out_gain)).astype(jnp.bfloat16)


def solution(mesh):
    in_specs = (
        P(("seq", "head"), None),
        P(),
        P(),
        P(None, "head"),
        P(),
        P("head", None),
        P(None, "seq", None),
        P("seq"),
        P(),
        P("seq"),
    )
    out_specs = P(("seq", "head"), None)
    return jax.shard_map(local, mesh=mesh, in_specs=in_specs, out_specs=out_specs, check_vma=False)
```

profile of v0, /device:TPU:0, one launch (start us, length us, event | category | flops | bytes accessed | tf_op | source)
XLA Modules:
  0.0 246.8 jit_solution(8027556891641300505)
XLA Ops:
  6.5 0.7 all-gather.10.cloned.1.call-update
  7.4 1.2 dynamic-slice
  9.2 0.8 convert_reduce_fusion
  10.0 0.2 dynamic-update-slice
  10.2 0.7 fusion.40
  11.0 0.2 dynamic-update-slice.1
  11.2 10.6 %all-reduce.2 = (s32[512]{0:T(512)S(1)}, s32[512]{0:T(512)S(1)}) all-reduce(s32[512]{0:T(512)S(1)} %dynamic-update-slice, s32[512]{0:T(512)S(1)} %dynamic-update-slice.1), channel_id=2, replica_groups=mesh['seq'=8,'head'=4] {'seq'}, use_global_device_ids=true, to_apply=%add | all-reduce | flops 1024 | bytes 8192
  22.2 0.1 reduce.2
  22.3 0.3 while.44
  22.6 0.7 subtract_subtract_fusion
  23.3 0.8 select_reduce_fusion
  24.1 25.3 %all-gather.10.cloned.1.call-done = bf16[512,2304]{1,0:T(8,128)(2,1)} async-done(((bf16[128,2304]{1,0:T(8,128)(2,1)}), bf16[512,2304]{1,0:T(8,128)(2,1)}) %all-gather.10.cloned.1.call-update) | async-done | bytes 2359312 | tf_op jit(solution)/shard_map/all_gather | solution.py:147
  49.4 2.2 fusion.28
  51.6 3.9 %fusion.31 = f32[512,512]{0,1:T(8,128)S(1)} fusion(bf16[2304,2048]{1,0:T(8,128)(2,1)} %param.20, s32[]{:T(128)S(6)} %select_n.68, bf16[512,2304]{1,0:T(8,128)(2,1)} %all-gather.10.cloned.1.call-done, f32[2304]{0:T(1024)} %param.17, f32[512]{0:T(512)S(1)} %add_rsqrt_fusion), kind=kOutput, calls=%fused_computation.45 | convolution fusion | flops 1212678144 | bytes 5781508 | tf_op jit(solution)/shard_map/dot_general | solution.py:154
  55.6 1.2 multiply_cosine_fusion
  56.8 0.8 pad_maximum_fusion
  57.7 1.7 constant_dynamic-slice_fusion.3
  59.6 12.9 %all-gather.4 = s32[8,1,512]{2,1,0:T(1,128)S(1)} all-gather(s32[1,1,512]{2,1,0:T(1,128)S(1)} %bitcast.98), channel_id=1, replica_groups=mesh['seq'=8,'head'=4] {'seq'}, dimensions={0}, use_global_device_ids=true | all-gather | bytes 18432 | tf_op jit(solution)/shard_map/all_gather | solution.py:172
  72.5 12.9 %all-gather.3 = s32[8,1,512]{2,1,0:T(1,128)S(1)} all-gather(s32[1,1,512]{2,1,0:T(1,128)S(1)} %bitcast.97), channel_id=1, replica_groups=mesh['seq'=8,'head'=4] {'seq'}, dimensions={0}, use_global_device_ids=true | all-gather | bytes 18432 | tf_op jit(solution)/shard_map/all_gather | solution.py:171
  85.5 0.2 select_reduce_fusion.2
  85.9 9.6 %all-gather.5 = s32[8,1,256]{2,1,0:T(1,128)S(1)} all-gather(s32[1,1,256]{2,1,0:T(1,128)S(1)} %reshape.296), channel_id=1, replica_groups=mesh['seq'=8,'head'=4] {'seq'}, dimensions={0}, use_global_device_ids=true | all-gather | bytes 9216 | tf_op jit(solution)/shard_map/all_gather | solution.py:180
  95.5 0.8 copy.41
  96.3 0.8 copy.43
  97.1 3.9 %fusion.34 = f32[512,512]{0,1:T(8,128)S(1)} fusion(bf16[2304,512]{1,0:T(8,128)(2,1)} %param.19, bf16[512,2304]{1,0:T(8,128)(2,1)} %all-gather.10.cloned.1.call-done, f32[2304]{0:T(1024)S(1)} %copy-done.9, f32[512]{0:T(512)S(1)} %add_rsqrt_fusion), kind=kOutput, calls=%fused_computation.52 | convolution fusion | flops 1212678144 | bytes 5778432 | tf_op jit(solution)/shard_map/dot_general | solution.py:150
  101.0 0.9 fusion.42
  101.9 0.2 copy.49
  102.1 1.2 copy.50
  103.4 1.1 multiply_subtract_fusion
  104.5 0.9 fusion.33
  105.4 6.5 %copy.48 = bf16[4096,512]{1,0:T(8,128)(2,1)} copy(bf16[4096,512]{0,1:T(8,128)(2,1)} %all-gather.12.cloned.1.call-done) | data formatting | bytes 8388608
  111.8 48.7 %while.45 = (s32[]{:T(128)}, f32[512,2,256]{2,0,1:T(8,128)}, f32[512,2]{0,1:T(2,128)S(1)}, s32[4,1024]{1,0:T(4,128)S(1)}, s32[512]{0:T(512)S(1)}, /*index=5*/s32...) while((s32[]{:T(128)}, f32[512,2,256]{2,0,1:T(8,128)}, ...), condition=%wide.region_9.10_spmd.clone, body=%wide.region_7.9_spmd.clone.sunk | while | flops 1084753408 | bytes 17873576 | solution.py:89
  111.9 1.1 and_and_fusion.5
  112.9 1.5 dynamic-slice_bitcast_fusion.5
  114.5 4.5 %fusion.63 = (f32[512,2]{0,1:T(2,128)S(1)}, f32[1024,512,2]{1,0,2:T(8,128)}) fusion(pred[512,1024]{0,1:T(8,128)(4,1)S(1)} %and_and_fusion.5, bf16[512,2,256]{2,0,1:T(8,128)(2,1)} %get-tuple-element.669, bf16[1024,512]{1,0:T(8,128)(2,1)S(1)} %dynamic-slice_bitcast_fusion.5), kind=kOutput, calls=%fused_computation.23.clone.1 | convolution fusion | flops 541064192 | bytes 5771264 | tf_op jit(solution)/shard_map/while/body/eval_jaxpr/qhd,kd->qhk/dot_general | solution.py:60
  119.0 4.8 %fusion.64 = f32[512,2,256]{2,0,1:T(8,128)} fusion(f32[1024,512,2]{1,0,2:T(8,128)} %get-tuple-element.611, pred[512,1024]{0,1:T(8,128)(4,1)} %copy-done.1, f32[512,2,256]{2,0,1:T(8,128)} %get-tuple-element.650, bf16[1024,512]{1,0:T(8,128)(2,1)S(1)} %dynamic-slice_bitcast_fusion.5, pred[]{:T(512)S(6)} %compare.9), kind=kOutput, calls=%fused_computation.28.clone.1 | convolution fusion | flops 541589504 | bytes 7340033 | tf_op jit(solution)/shard_map/while/body/eval_jaxpr/qhk,kd->qhd/dot_general | solution.py:71
  123.9 1.1 and_and_fusion.5
  124.9 1.5 dynamic-slice_bitcast_fusion.5
  126.4 4.5 %fusion.63 = (f32[512,2]{0,1:T(2,128)S(1)}, f32[1024,512,2]{1,0,2:T(8,128)}) fusion(pred[512,1024]{0,1:T(8,128)(4,1)S(1)} %and_and_fusion.5, bf16[512,2,256]{2,0,1:T(8,128)(2,1)} %get-tuple-element.669, bf16[1024,512]{1,0:T(8,128)(2,1)S(1)} %dynamic-slice_bitcast_fusion.5), kind=kOutput, calls=%fused_computation.23.clone.1 | convolution fusion | flops 541064192 | bytes 5771264 | tf_op jit(solution)/shard_map/while/body/eval_jaxpr/qhd,kd->qhk/dot_general | solution.py:60
  131.0 5.1 %fusion.64 = f32[512,2,256]{2,0,1:T(8,128)} fusion(f32[1024,512,2]{1,0,2:T(8,128)} %get-tuple-element.611, pred[512,1024]{0,1:T(8,128)(4,1)} %copy-done.1, f32[512,2,256]{2,0,1:T(8,128)} %get-tuple-element.650, bf16[1024,512]{1,0:T(8,128)(2,1)S(1)} %dynamic-slice_bitcast_fusion.5, pred[]{:T(512)S(6)} %compare.9), kind=kOutput, calls=%fused_computation.28.clone.1 | convolution fusion | flops 541589504 | bytes 7340033 | tf_op jit(solution)/shard_map/while/body/eval_jaxpr/qhk,kd->qhd/dot_general | solution.py:71
  136.1 1.1 and_and_fusion.5
  137.2 1.5 dynamic-slice_bitcast_fusion.5
  138.7 4.5 %fusion.63 = (f32[512,2]{0,1:T(2,128)S(1)}, f32[1024,512,2]{1,0,2:T(8,128)}) fusion(pred[512,1024]{0,1:T(8,128)(4,1)S(1)} %and_and_fusion.5, bf16[512,2,256]{2,0,1:T(8,128)(2,1)} %get-tuple-element.669, bf16[1024,512]{1,0:T(8,128)(2,1)S(1)} %dynamic-slice_bitcast_fusion.5), kind=kOutput, calls=%fused_computation.23.clone.1 | convolution fusion | flops 541064192 | bytes 5771264 | tf_op jit(solution)/shard_map/while/body/eval_jaxpr/qhd,kd->qhk/dot_general | solution.py:60
  143.2 5.1 %fusion.64 = f32[512,2,256]{2,0,1:T(8,128)} fusion(f32[1024,512,2]{1,0,2:T(8,128)} %get-tuple-element.611, pred[512,1024]{0,1:T(8,128)(4,1)} %copy-done.1, f32[512,2,256]{2,0,1:T(8,128)} %get-tuple-element.650, bf16[1024,512]{1,0:T(8,128)(2,1)S(1)} %dynamic-slice_bitcast_fusion.5, pred[]{:T(512)S(6)} %compare.9), kind=kOutput, calls=%fused_computation.28.clone.1 | convolution fusion | flops 541589504 | bytes 7340033 | tf_op jit(solution)/shard_map/while/body/eval_jaxpr/qhk,kd->qhd/dot_general | solution.py:71
  148.4 1.1 and_and_fusion.5
  149.4 1.5 dynamic-slice_bitcast_fusion.5
  150.9 4.5 %fusion.63 = (f32[512,2]{0,1:T(2,128)S(1)}, f32[1024,512,2]{1,0,2:T(8,128)}) fusion(pred[512,1024]{0,1:T(8,128)(4,1)S(1)} %and_and_fusion.5, bf16[512,2,256]{2,0,1:T(8,128)(2,1)} %get-tuple-element.669, bf16[1024,512]{1,0:T(8,128)(2,1)S(1)} %dynamic-slice_bitcast_fusion.5), kind=kOutput, calls=%fused_computation.23.clone.1 | convolution fusion | flops 541064192 | bytes 5771264 | tf_op jit(solution)/shard_map/while/body/eval_jaxpr/qhd,kd->qhk/dot_general | solution.py:60
  155.5 5.1 %fusion.64 = f32[512,2,256]{2,0,1:T(8,128)} fusion(f32[1024,512,2]{1,0,2:T(8,128)} %get-tuple-element.611, pred[512,1024]{0,1:T(8,128)(4,1)} %copy-done.1, f32[512,2,256]{2,0,1:T(8,128)} %get-tuple-element.650, bf16[1024,512]{1,0:T(8,128)(2,1)S(1)} %dynamic-slice_bitcast_fusion.5, pred[]{:T(512)S(6)} %compare.9), kind=kOutput, calls=%fused_computation.28.clone.1 | convolution fusion | flops 541589504 | bytes 7340033 | tf_op jit(solution)/shard_map/while/body/eval_jaxpr/qhk,kd->qhd/dot_general | solution.py:71
  160.6 14.8 %while.43 = (s32[]{:T(128)}, f32[512,2,256]{2,0,1:T(8,128)}, f32[512,2]{0,1:T(2,128)S(1)}, s32[2,1024]{1,0:T(2,128)S(1)}, s32[512]{0:T(512)S(1)}, /*index=5*/pre...) while((s32[]{:T(128)}, f32[512,2,256]{2,0,1:T(8,128)}, ...), condition=%wide.region_15.16_spmd.clone, body=%wide.region_13.15_spmd.clone.sunk | while | flops 1083966464 | bytes 24149672 | solution.py:89
  160.6 0.5 and_and_fusion.4
  161.1 1.3 dynamic-slice_bitcast_fusion.4
  162.4 2.7 %fusion.59 = (f32[512,2]{0,1:T(2,128)S(1)}, f32[1024,512,2]{1,0,2:T(8,128)S(1)}) fusion(pred[512,1024]{0,1:T(8,128)(4,1)S(1)} %and_and_fusion.4, bf16[512,2,256]{2,0,1:T(8,128)(2,1)} %get-tuple-element.700, bf16[1024,512]{1,0:T(8,128)(2,1)S(1)} %dynamic-slice_bitcast_fusion.4), kind=kOutput, calls=%fused_computation.3.clone.1 | convolution fusion | flops 541064192 | bytes 5771264 | tf_op jit(solution)/shard_map/while/body/eval_jaxpr/qhd,kd->qhk/dot_general | solution.py:60
  165.2 1.8 fusion.60
  167.1 0.9 copy-done.4
  168.0 0.5 and_and_fusion.4
  168.5 1.3 dynamic-slice_bitcast_fusion.4
  169.8 2.7 %fusion.59 = (f32[512,2]{0,1:T(2,128)S(1)}, f32[1024,512,2]{1,0,2:T(8,128)S(1)}) fusion(pred[512,1024]{0,1:T(8,128)(4,1)S(1)} %and_and_fusion.4, bf16[512,2,256]{2,0,1:T(8,128)(2,1)} %get-tuple-element.700, bf16[1024,512]{1,0:T(8,128)(2,1)S(1)} %dynamic-slice_bitcast_fusion.4), kind=kOutput, calls=%fused_computation.3.clone.1 | convolution fusion | flops 541064192 | bytes 5771264 | tf_op jit(solution)/shard_map/while/body/eval_jaxpr/qhd,kd->qhk/dot_general | solution.py:60
  172.6 1.9 fusion.60
  174.5 0.9 copy-done.4
  175.4 1.6 copy.45
  177.0 0.1 select_convert_fusion
  177.1 3.5 %fusion.43 = f32[512,2304]{1,0:T(8,128)} fusion(bf16[512,512]{0,1:T(8,128)(2,1)S(1)} %bitcast.92, bf16[512,2304]{1,0:T(8,128)(2,1)S(1)} %copy-done), kind=kOutput, calls=%fused_computation.85 | convolution fusion | flops 1207959552 | bytes 7602176 | tf_op jit(solution)/shard_map/dot_general | solution.py:190
  180.7 55.8 %reduce-scatter.2.cloned.1.call-done = f32[128,2304]{1,0:T(8,128)} async-done(((f32[512,2304]{1,0:T(8,128)}), f32[128,2304]{1,0:T(8,128)}) %reduce-scatter.2.cloned.1.call-update) | async-done | bytes 1179664 | tf_op jit(solution)/shard_map/reduce_scatter | solution.py:189
  236.5 1.4 multiply_reduce_fusion
  237.9 2.3 add_convert_fusion
  (93 shorter events, 1.4 us)
Async XLA Ops:
  6.5 170.6 %copy-start = (bf16[512,2304]{1,0:T(8,128)(2,1)S(1)}, bf16[512,2304]{1,0:T(8,128)(2,1)}, u32[]{:S(2)}) copy-start(bf16[512,2304]{1,0:T(8,128)(2,1)} %param.21) | copy-start | bytes 7077892
  6.5 42.9 %all-gather.10.cloned.1.call-start = ((), (), s32[]{:S(2)}) async-start(), calls=%async_computation.1 | async-start | bytes 2949120 | tf_op jit(solution)/shard_map/all_gather | solution.py:147
  7.3 98.1 %all-gather.12.cloned.1.call-start = ((), (), s32[]{:S(2)}) async-start(), calls=%async_computation.2 | async-start | bytes 4718592 | tf_op jit(solution)/shard_map/all_gather | solution.py:170
  55.5 3.9 %copy-start.5 = (s32[512]{0:T(512)S(1)}, s32[512]{0:T(512)}, u32[]{:S(2)}) copy-start(s32[512]{0:T(512)} %param.23) | copy-start | bytes 6148
  55.6 4.0 %copy-start.7 = (s32[16]{0:T(128)S(1)}, s32[16]{0:T(128)}, u32[]{:S(2)}) copy-start(s32[16]{0:T(128)} %param.25) | copy-start | bytes 196
  55.6 29.9 %copy-start.8 = (s32[64]{0:T(128)S(1)}, s32[64]{0:T(128)}, u32[]{:S(2)}) copy-start(s32[64]{0:T(128)} %param.24) | copy-start | bytes 772
  55.6 41.6 %copy-start.9 = (f32[2304]{0:T(1024)S(1)}, f32[2304]{0:T(1024)}, u32[]{:S(2)}) copy-start(f32[2304]{0:T(1024)} %param.17) | copy-start | bytes 27652
  57.7 102.9 %all-gather.14.cloned.1.call-start = ((), (), s32[]{:S(2)}) async-start(), calls=%async_computation.4 | async-start | bytes 2359296 | tf_op jit(solution)/shard_map/all_gather | solution.py:179
  59.4 177.1 %reduce-scatter.2.cloned.1.call-start = ((), (), s32[]{:S(2)}) async-start(), calls=%async_computation.3 | async-start | bytes 5898240 | tf_op jit(solution)/shard_map/reduce_scatter | solution.py:189
  112.9 6.1 %copy-start.1 = (pred[512,1024]{0,1:T(8,128)(4,1)}, pred[512,1024]{0,1:T(8,128)(4,1)S(1)}, u32[]{:S(2)}) copy-start(pred[512,1024]{0,1:T(8,128)(4,1)S(1)} %and_and_fusion.5) | copy-start | bytes 1572868 | tf_op jit(solution)/shard_map/while
  124.9 6.0 %copy-start.1 = (pred[512,1024]{0,1:T(8,128)(4,1)}, pred[512,1024]{0,1:T(8,128)(4,1)S(1)}, u32[]{:S(2)}) copy-start(pred[512,1024]{0,1:T(8,128)(4,1)S(1)} %and_and_fusion.5) | copy-start | bytes 1572868 | tf_op jit(solution)/shard_map/while
  137.2 6.0 %copy-start.1 = (pred[512,1024]{0,1:T(8,128)(4,1)}, pred[512,1024]{0,1:T(8,128)(4,1)S(1)}, u32[]{:S(2)}) copy-start(pred[512,1024]{0,1:T(8,128)(4,1)S(1)} %and_and_fusion.5) | copy-start | bytes 1572868 | tf_op jit(solution)/shard_map/while
  149.4 6.0 %copy-start.1 = (pred[512,1024]{0,1:T(8,128)(4,1)}, pred[512,1024]{0,1:T(8,128)(4,1)S(1)}, u32[]{:S(2)}) copy-start(pred[512,1024]{0,1:T(8,128)(4,1)S(1)} %and_and_fusion.5) | copy-start | bytes 1572868 | tf_op jit(solution)/shard_map/while
  162.4 2.7 %copy-start.3 = (f32[512,2,256]{2,0,1:T(8,128)S(1)}, f32[512,2,256]{2,0,1:T(8,128)}, u32[]{:S(2)}) copy-start(f32[512,2,256]{2,0,1:T(8,128)} %get-tuple-element.684) | copy-start | bytes 3145732 | tf_op jit(solution)/shard_map/while
  167.0 1.0 copy-start.4
  169.8 2.7 %copy-start.3 = (f32[512,2,256]{2,0,1:T(8,128)S(1)}, f32[512,2,256]{2,0,1:T(8,128)}, u32[]{:S(2)}) copy-start(f32[512,2,256]{2,0,1:T(8,128)} %get-tuple-element.684) | copy-start | bytes 3145732 | tf_op jit(solution)/shard_map/while
  174.4 1.0 copy-start.4
  180.7 57.2 %copy-start.2 = (bf16[128,2304]{1,0:T(8,128)(2,1)S(1)}, bf16[128,2304]{1,0:T(8,128)(2,1)}, u32[]{:S(2)}) copy-start(bf16[128,2304]{1,0:T(8,128)(2,1)} %param.16) | copy-start | bytes 1769476
  180.7 57.3 %copy-start.6 = (f32[2304]{0:T(1024)S(1)}, f32[2304]{0:T(1024)}, u32[]{:S(2)}) copy-start(f32[2304]{0:T(1024)} %param.18) | copy-start | bytes 27652
Sparse Core Ops, SparseCore 0:
  9.2 40.1 all-gather.9
  57.8 47.2 all-gather.11
  106.7 27.8 all-gather.13
  180.8 55.6 reduce-scatter.1
where the time goes:
time: 248 us; the launch traced here: 247 us
  waiting for transfers between devices  81.9 us (33%)
  matrix products  58.7 us (24%)
  blocking collectives  45.9 us (19%)
  local copies, waits for them, and re-layouts  26.4 us (11%)
  other arithmetic  19.2 us (8%)
  between operations  14 us (6%)
    reduce_scatter x1, waiting for transfers between devices, local(): lax.psum_scatter(jnp.dot(attended, out_weight, preferred_element_type=jnp...  55.8 us
    all_gather x1, waiting for transfers between devices, local(): portion = lax.all_gather(tokens, 'head', axis=0, tiled=True)  25.3 us
    dot_general x6, matrix products, advance(): jnp.einsum('qhk,kd->qhd', weights.astype(jnp.bfloat16), pair_rows[:, key_...  23.7 us
    dot_general x6, matrix products, advance(): jnp.einsum('qhd,kd->qhk', queries, pair_rows[:, :key_width], preferred_el...  23.6 us
    all_gather x1, blocking collectives, local(): lax.all_gather(segment_ids, 'seq', axis=0, tiled=True)  12.9 us
    all_gather x1, blocking collectives, local(): lax.all_gather(q_slot, 'seq', axis=0, tiled=True)  12.9 us
    unnamed x1, blocking collectives  10.6 us
    unnamed x21, local copies, waits for them, and re-layouts  9.73 us
  transfers between devices with their start and end apart: 4, of which 2 were waited for; matrix products, arithmetic and copies ran while one was open for 29% of the time, Pallas kernels for 0%

commit v1 on v0

--- a/solution.py
+++ b/solution.py
@@ -11,6 +11,17 @@
 BLK = 16
 EPSILON = 1e-06
 SOFT_CAP = 50.0
+
+
+def turned_line(value, name, dim):
+    size = lax.axis_size(name)
+    right = [(i, (i + 1) % size) for i in range(size)]
+    pieces = [value]
+    for stride in range(1, size):
+        pieces = [lax.ppermute(pieces[0], name, right), *pieces]
+    full = jnp.concatenate(pieces, axis=dim)
+    shift = (lax.axis_index(name) + 1) * pieces[-1].shape[dim]
+    return jnp.roll(full, shift, axis=dim)
 
 
 def carried_in(array, axis, combine, identity):
@@ -144,7 +155,7 @@
     cache_pairs = lax.dynamic_index_in_dim(cache_entries, shared_head, 0, keepdims=False)
     cache_slot = jnp.full((cache_seg.shape[0],), -1, jnp.int32)
     w_shared = lax.dynamic_slice_in_dim(keyval_weight, shared_head * 2 * HD, 2 * HD, 1)
-    portion = lax.all_gather(tokens, "head", axis=0, tiled=True)
+    portion = turned_line(tokens, "head", 0)
     row_count = portion.shape[0]
     normed = rms_scale(portion, in_gain).astype(jnp.bfloat16)
     query_rows = jnp.dot(normed, query_weight, preferred_element_type=jnp.float32).reshape(

time: 248 us -> 260 us (1.048)
  local copies, waits for them, and re-layouts: 26.4 us -> 36.5 us
  starting transfers between devices: 0.12 us -> 4.81 us
  waiting for transfers between devices: 81.9 us -> 77.8 us
    all_gather x1 -> x0, waiting for transfers between devices: 25.3 us -> none  [local(): portion = lax.all_gather(tokens, 'head', axis=0, tiled=True)]
    ppermute x0 -> x3, waiting for transfers between devices: none -> 22.3 us  [turned_line(): pieces = [lax.ppermute(pieces[0], name, right), *pieces]]
    unnamed x21 -> x36, local copies, waits for them, and re-layouts: 9.73 us -> 15.3 us
    ppermute x0 -> x3, starting transfers between devices: none -> 4.73 us  [turned_line(): pieces = [lax.ppermute(pieces[0], name, right), *pieces]]
  transfers between devices with their start and end apart: 4 -> 6, of which waited for: 2 -> 3; matrix products, arithmetic and copies ran while one was open for 29% -> 31% of each run, Pallas kernels for 0% -> 0%
where the time goes in v1:
time: 260 us; the launch traced here: 258 us
  waiting for transfers between devices  77.8 us (30%)
  matrix products  59.1 us (23%)
  blocking collectives  44.5 us (17%)
  local copies, waits for them, and re-layouts  36.5 us (14%)
  other arithmetic  21 us (8%)
  between operations  14.1 us (5%)
  starting transfers between devices  4.81 us (2%)
    reduce_scatter x1, waiting for transfers between devices, local(): lax.psum_scatter(jnp.dot(attended, out_weight, preferred_element_type=jnp...  55.4 us
    dot_general x6, matrix products, advance(): jnp.einsum('qhk,kd->qhd', weights.astype(jnp.bfloat16), pair_rows[:, key_...  23.7 us
    dot_general x6, matrix products, advance(): jnp.einsum('qhd,kd->qhk', queries, pair_rows[:, :key_width], preferred_el...  23.6 us
    ppermute x3, waiting for transfers between devices, turned_line(): pieces = [lax.ppermute(pieces[0], name, right), *pieces]  22.3 us
    unnamed x36, local copies, waits for them, and re-layouts  15.3 us
    all_gather x1, blocking collectives, local(): lax.all_gather(segment_ids, 'seq', axis=0, tiled=True)  13 us
    all_gather x1, blocking collectives, local(): lax.all_gather(q_slot, 'seq', axis=0, tiled=True)  12.8 us
    unnamed x1, blocking collectives  9.76 us
  transfers between devices with their start and end apart: 6, of which 3 were waited for; matrix products, arithmetic and copies ran while one was open for 31% of the time, Pallas kernels for 0%

profile of v1, /device:TPU:0, one launch (start us, length us, event | category | flops | bytes accessed | tf_op | source)
XLA Modules:
  0.0 258.2 jit_solution(16121590005140627763)
XLA Ops:
  6.5 2.9 %collective-permute-start = (bf16[128,2304]{1,0:T(8,128)(2,1)}, bf16[128,2304]{1,0:T(8,128)(2,1)S(1)}, u32[]{:S(2)}, u32[]{:S(2)}) collective-permute-start(bf16[128,2304]{1,0:T(8,128)(2,1)} %param.16), channel_id=1, source_target_pairs={{0,1},{1,2},{2,3},{3,0},{4,5},{5,6},{6,7},{7,4},{8,9},{9,10},{10,1... | collective-permute-start | bytes 1769480 | tf_op jit(solution)/shard_map/ppermute | solution.py:21
  9.5 1.2 dynamic-slice
  11.4 0.8 convert_reduce_fusion
  12.8 1.3 fusion.40
  14.1 0.9 dynamic-update-slice.1
  15.0 9.8 %all-reduce.2 = (s32[512]{0:T(512)}, s32[512]{0:T(512)}) all-reduce(s32[512]{0:T(512)S(1)} %dynamic-update-slice, s32[512]{0:T(512)S(1)} %dynamic-update-slice.1), channel_id=2, replica_groups=mesh['seq'=8,'head'=4] {'seq'}, use_global_device_ids=true, to_apply=%add | all-reduce | flops 1024 | bytes 8192
  25.5 0.8 reshape.283
  26.2 1.5 collective-permute-start.1
  28.0 13.3 %collective-permute-done.1 = bf16[128,2304]{1,0:T(8,128)(2,1)} collective-permute-done((bf16[128,2304]{1,0:T(8,128)(2,1)S(1)}, bf16[128,2304]{1,0:T(8,128)(2,1)}, u32[]{:S(2)}, u32[]{:S(2)}) %collective-permute-start.1) | collective-permute-done | bytes 589856 | tf_op jit(solution)/shard_map/ppermute | solution.py:21
  41.7 1.4 copy.39
  43.0 1.4 reduce-window.9
  44.5 0.9 reduce.2
  46.0 0.8 select_reduce_fusion
  46.8 9.0 %collective-permute-done.2 = bf16[128,2304]{1,0:T(8,128)(2,1)} collective-permute-done((bf16[128,2304]{1,0:T(8,128)(2,1)}, bf16[128,2304]{1,0:T(8,128)(2,1)}, u32[]{:S(2)}, u32[]{:S(2)}) %collective-permute-start.2) | collective-permute-done | bytes 589856 | tf_op jit(solution)/shard_map/ppermute | solution.py:21
  55.7 1.1 constant_dynamic-update-slice_fusion.7
  56.9 1.1 constant_dynamic-update-slice_fusion.6
  58.1 1.1 constant_dynamic-update-slice_fusion.3
  59.2 1.1 constant_dynamic-update-slice_fusion.2
  61.0 4.3 %fusion.31 = f32[512,512]{0,1:T(8,128)S(1)} fusion(bf16[2304,2048]{1,0:T(8,128)(2,1)} %param.20, s32[]{:T(128)S(6)} %select_n.82, f32[2304]{0:T(1024)S(1)} %copy-done.12, f32[512]{0:T(512)S(1)} %add_rsqrt_fusion, bf16[1024,2304]{1,0:T(8,128)(2,1)S(1)} %constant_dynamic-update-slice_fusion, s32[]{:T(128)S(6)} %select_n.80), kind=kOutput, calls=%fused_computation.45 | convolution fusion | flops 1212678144 | bytes 5781512 | tf_op jit(solution)/shard_map/dot_general | solution.py:165
  65.4 1.9 multiply_cosine_fusion
  67.3 0.8 pad_maximum_fusion
  68.2 1.7 constant_dynamic-slice_fusion.3
  70.1 12.8 %all-gather.4 = s32[8,1,512]{2,1,0:T(1,128)S(1)} all-gather(s32[1,1,512]{2,1,0:T(1,128)S(1)} %bitcast.98), channel_id=1, replica_groups=mesh['seq'=8,'head'=4] {'seq'}, dimensions={0}, use_global_device_ids=true | all-gather | bytes 18432 | tf_op jit(solution)/shard_map/all_gather | solution.py:183
  83.0 13.0 %all-gather.3 = s32[8,1,512]{2,1,0:T(1,128)S(1)} all-gather(s32[1,1,512]{2,1,0:T(1,128)S(1)} %bitcast.97), channel_id=1, replica_groups=mesh['seq'=8,'head'=4] {'seq'}, dimensions={0}, use_global_device_ids=true | all-gather | bytes 18432 | tf_op jit(solution)/shard_map/all_gather | solution.py:182
  96.4 8.9 %all-gather.5 = s32[8,1,256]{2,1,0:T(1,128)S(1)} all-gather(s32[1,1,256]{2,1,0:T(1,128)S(1)} %reshape.296), channel_id=1, replica_groups=mesh['seq'=8,'head'=4] {'seq'}, dimensions={0}, use_global_device_ids=true | all-gather | bytes 9216 | tf_op jit(solution)/shard_map/all_gather | solution.py:191
  105.4 3.9 %fusion.34 = f32[512,512]{0,1:T(8,128)S(1)} fusion(bf16[2304,512]{1,0:T(8,128)(2,1)} %param.19, f32[2304]{0:T(1024)S(1)} %copy-done.13, f32[512]{0:T(512)S(1)} %add_rsqrt_fusion, bf16[1024,2304]{1,0:T(8,128)(2,1)} %copy-done.4, s32[]{:T(128)S(6)} %select_n.80), kind=kOutput, calls=%fused_computation.56 | convolution fusion | flops 1212678144 | bytes 5778436 | tf_op jit(solution)/shard_map/dot_general | solution.py:161
  109.3 0.9 fusion.43
  110.4 1.2 copy.50
  111.6 1.8 copy.41
  113.4 1.8 copy.43
  115.2 1.1 multiply_subtract_fusion
  116.4 0.9 fusion.33
  117.2 6.5 %copy.48 = bf16[4096,512]{1,0:T(8,128)(2,1)} copy(bf16[4096,512]{0,1:T(8,128)(2,1)} %all-gather.9.cloned.1.call-done) | data formatting | bytes 8388608
  123.7 48.6 %while.45 = (s32[]{:T(128)}, f32[512,2,256]{2,0,1:T(8,128)}, f32[512,2]{0,1:T(2,128)S(1)}, s32[4,1024]{1,0:T(4,128)S(1)}, s32[512]{0:T(512)S(1)}, /*index=5*/s32...) while((s32[]{:T(128)}, f32[512,2,256]{2,0,1:T(8,128)}, ...), condition=%wide.region_9.10_spmd.clone, body=%wide.region_7.9_spmd.clone.sunk | while | flops 1084753408 | bytes 17873576 | solution.py:100
  123.7 1.1 and_and_fusion.5
  124.8 1.5 dynamic-slice_bitcast_fusion.5
  126.3 4.5 %fusion.64 = (f32[512,2]{0,1:T(2,128)S(1)}, f32[1024,512,2]{1,0,2:T(8,128)}) fusion(pred[512,1024]{0,1:T(8,128)(4,1)S(1)} %and_and_fusion.5, bf16[512,2,256]{2,0,1:T(8,128)(2,1)} %get-tuple-element.669, bf16[1024,512]{1,0:T(8,128)(2,1)S(1)} %dynamic-slice_bitcast_fusion.5), kind=kOutput, calls=%fused_computation.23.clone.1 | convolution fusion | flops 541064192 | bytes 5771264 | tf_op jit(solution)/shard_map/while/body/eval_jaxpr/qhd,kd->qhk/dot_general | solution.py:71
  130.9 4.8 %fusion.65 = f32[512,2,256]{2,0,1:T(8,128)} fusion(f32[1024,512,2]{1,0,2:T(8,128)} %get-tuple-element.611, pred[512,1024]{0,1:T(8,128)(4,1)} %copy-done.1, f32[512,2,256]{2,0,1:T(8,128)} %get-tuple-element.650, bf16[1024,512]{1,0:T(8,128)(2,1)S(1)} %dynamic-slice_bitcast_fusion.5, pred[]{:T(512)S(6)} %compare.10), kind=kOutput, calls=%fused_computation.28.clone.1 | convolution fusion | flops 541589504 | bytes 7340033 | tf_op jit(solution)/shard_map/while/body/eval_jaxpr/qhk,kd->qhd/dot_general | solution.py:82
  135.7 1.1 and_and_fusion.5
  136.8 1.5 dynamic-slice_bitcast_fusion.5
  138.3 4.5 %fusion.64 = (f32[512,2]{0,1:T(2,128)S(1)}, f32[1024,512,2]{1,0,2:T(8,128)}) fusion(pred[512,1024]{0,1:T(8,128)(4,1)S(1)} %and_and_fusion.5, bf16[512,2,256]{2,0,1:T(8,128)(2,1)} %get-tuple-element.669, bf16[1024,512]{1,0:T(8,128)(2,1)S(1)} %dynamic-slice_bitcast_fusion.5), kind=kOutput, calls=%fused_computation.23.clone.1 | convolution fusion | flops 541064192 | bytes 5771264 | tf_op jit(solution)/shard_map/while/body/eval_jaxpr/qhd,kd->qhk/dot_general | solution.py:71
  142.8 5.1 %fusion.65 = f32[512,2,256]{2,0,1:T(8,128)} fusion(f32[1024,512,2]{1,0,2:T(8,128)} %get-tuple-element.611, pred[512,1024]{0,1:T(8,128)(4,1)} %copy-done.1, f32[512,2,256]{2,0,1:T(8,128)} %get-tuple-element.650, bf16[1024,512]{1,0:T(8,128)(2,1)S(1)} %dynamic-slice_bitcast_fusion.5, pred[]{:T(512)S(6)} %compare.10), kind=kOutput, calls=%fused_computation.28.clone.1 | convolution fusion | flops 541589504 | bytes 7340033 | tf_op jit(solution)/shard_map/while/body/eval_jaxpr/qhk,kd->qhd/dot_general | solution.py:82
  147.9 1.1 and_and_fusion.5
  149.0 1.5 dynamic-slice_bitcast_fusion.5
  150.5 4.5 %fusion.64 = (f32[512,2]{0,1:T(2,128)S(1)}, f32[1024,512,2]{1,0,2:T(8,128)}) fusion(pred[512,1024]{0,1:T(8,128)(4,1)S(1)} %and_and_fusion.5, bf16[512,2,256]{2,0,1:T(8,128)(2,1)} %get-tuple-element.669, bf16[1024,512]{1,0:T(8,128)(2,1)S(1)} %dynamic-slice_bitcast_fusion.5), kind=kOutput, calls=%fused_computation.23.clone.1 | convolution fusion | flops 541064192 | bytes 5771264 | tf_op jit(solution)/shard_map/while/body/eval_jaxpr/qhd,kd->qhk/dot_general | solution.py:71
  155.0 5.1 %fusion.65 = f32[512,2,256]{2,0,1:T(8,128)} fusion(f32[1024,512,2]{1,0,2:T(8,128)} %get-tuple-element.611, pred[512,1024]{0,1:T(8,128)(4,1)} %copy-done.1, f32[512,2,256]{2,0,1:T(8,128)} %get-tuple-element.650, bf16[1024,512]{1,0:T(8,128)(2,1)S(1)} %dynamic-slice_bitcast_fusion.5, pred[]{:T(512)S(6)} %compare.10), kind=kOutput, calls=%fused_computation.28.clone.1 | convolution fusion | flops 541589504 | bytes 7340033 | tf_op jit(solution)/shard_map/while/body/eval_jaxpr/qhk,kd->qhd/dot_general | solution.py:82
  160.2 1.1 and_and_fusion.5
  161.2 1.5 dynamic-slice_bitcast_fusion.5
  162.7 4.5 %fusion.64 = (f32[512,2]{0,1:T(2,128)S(1)}, f32[1024,512,2]{1,0,2:T(8,128)}) fusion(pred[512,1024]{0,1:T(8,128)(4,1)S(1)} %and_and_fusion.5, bf16[512,2,256]{2,0,1:T(8,128)(2,1)} %get-tuple-element.669, bf16[1024,512]{1,0:T(8,128)(2,1)S(1)} %dynamic-slice_bitcast_fusion.5), kind=kOutput, calls=%fused_computation.23.clone.1 | convolution fusion | flops 541064192 | bytes 5771264 | tf_op jit(solution)/shard_map/while/body/eval_jaxpr/qhd,kd->qhk/dot_general | solution.py:71
  167.3 5.1 %fusion.65 = f32[512,2,256]{2,0,1:T(8,128)} fusion(f32[1024,512,2]{1,0,2:T(8,128)} %get-tuple-element.611, pred[512,1024]{0,1:T(8,128)(4,1)} %copy-done.1, f32[512,2,256]{2,0,1:T(8,128)} %get-tuple-element.650, bf16[1024,512]{1,0:T(8,128)(2,1)S(1)} %dynamic-slice_bitcast_fusion.5, pred[]{:T(512)S(6)} %compare.10), kind=kOutput, calls=%fused_computation.28.clone.1 | convolution fusion | flops 541589504 | bytes 7340033 | tf_op jit(solution)/shard_map/while/body/eval_jaxpr/qhk,kd->qhd/dot_general | solution.py:82
  172.4 14.8 %while.43 = (s32[]{:T(128)}, f32[512,2,256]{2,0,1:T(8,128)}, f32[512,2]{0,1:T(2,128)S(1)}, s32[2,1024]{1,0:T(2,128)S(1)}, s32[512]{0:T(512)S(1)}, /*index=5*/pre...) while((s32[]{:T(128)}, f32[512,2,256]{2,0,1:T(8,128)}, ...), condition=%wide.region_15.16_spmd.clone, body=%wide.region_13.15_spmd.clone.sunk | while | flops 1083966464 | bytes 24149672 | solution.py:100
  172.9 1.3 dynamic-slice_bitcast_fusion.4
  174.2 2.7 %fusion.60 = (f32[512,2]{0,1:T(2,128)S(1)}, f32[1024,512,2]{1,0,2:T(8,128)S(1)}) fusion(pred[512,1024]{0,1:T(8,128)(4,1)S(1)} %and_and_fusion.4, bf16[512,2,256]{2,0,1:T(8,128)(2,1)} %get-tuple-element.700, bf16[1024,512]{1,0:T(8,128)(2,1)S(1)} %dynamic-slice_bitcast_fusion.4), kind=kOutput, calls=%fused_computation.3.clone.1 | convolution fusion | flops 541064192 | bytes 5771264 | tf_op jit(solution)/shard_map/while/body/eval_jaxpr/qhd,kd->qhk/dot_general | solution.py:71
  177.0 1.9 fusion.61
  178.9 0.9 copy-done.6
  180.3 1.3 dynamic-slice_bitcast_fusion.4
  181.6 2.7 %fusion.60 = (f32[512,2]{0,1:T(2,128)S(1)}, f32[1024,512,2]{1,0,2:T(8,128)S(1)}) fusion(pred[512,1024]{0,1:T(8,128)(4,1)S(1)} %and_and_fusion.4, bf16[512,2,256]{2,0,1:T(8,128)(2,1)} %get-tuple-element.700, bf16[1024,512]{1,0:T(8,128)(2,1)S(1)} %dynamic-slice_bitcast_fusion.4), kind=kOutput, calls=%fused_computation.3.clone.1 | convolution fusion | flops 541064192 | bytes 5771264 | tf_op jit(solution)/shard_map/while/body/eval_jaxpr/qhd,kd->qhk/dot_general | solution.py:71
  184.4 1.9 fusion.61
  186.3 0.9 copy-done.6
  187.2 1.6 copy.45
  188.9 3.5 %fusion.44 = f32[512,2304]{1,0:T(8,128)} fusion(bf16[512,512]{0,1:T(8,128)(2,1)S(1)} %bitcast.92, bf16[512,2304]{1,0:T(8,128)(2,1)S(1)} %copy-done), kind=kOutput, calls=%fused_computation.94 | convolution fusion | flops 1207959552 | bytes 7602176 | tf_op jit(solution)/shard_map/dot_general | solution.py:201
  192.5 55.4 %reduce-scatter.2.cloned.1.call-done = f32[128,2304]{1,0:T(8,128)} async-done(((f32[512,2304]{1,0:T(8,128)}), f32[128,2304]{1,0:T(8,128)}) %reduce-scatter.2.cloned.1.call-update) | async-done | bytes 1179664 | tf_op jit(solution)/shard_map/reduce_scatter | solution.py:200
  247.9 1.4 multiply_reduce_fusion
  249.4 2.3 add_convert_fusion
  (112 shorter events, 5.8 us)
Async XLA Ops:
  6.5 182.4 %copy-start = (bf16[512,2304]{1,0:T(8,128)(2,1)S(1)}, bf16[512,2304]{1,0:T(8,128)(2,1)}, u32[]{:S(2)}) copy-start(bf16[512,2304]{1,0:T(8,128)(2,1)} %param.21) | copy-start | bytes 7077892
  6.5 51.5 %copy-start.2 = (bf16[128,2304]{1,0:T(8,128)(2,1)S(1)}, bf16[128,2304]{1,0:T(8,128)(2,1)}, u32[]{:S(2)}) copy-start(bf16[128,2304]{1,0:T(8,128)(2,1)} %param.16) | copy-start | bytes 1769476
  6.5 110.7 %all-gather.9.cloned.1.call-start = ((), (), s32[]{:S(2)}) async-start(), calls=%async_computation.1 | async-start | bytes 4718592 | tf_op jit(solution)/shard_map/all_gather | solution.py:181
  6.5 19.7 %collective-permute-start = (bf16[128,2304]{1,0:T(8,128)(2,1)}, bf16[128,2304]{1,0:T(8,128)(2,1)S(1)}, u32[]{:S(2)}, u32[]{:S(2)}) collective-permute-start(bf16[128,2304]{1,0:T(8,128)(2,1)} %param.16), channel_id=1, source_target_pairs={{0,1},{1,2},{2,3},{3,0},{4,5},{5,6},{6,7},{7,4},{8,9},{9,10},{10,1... | collective-permute-start | bytes 1769480 | tf_op jit(solution)/shard_map/ppermute | solution.py:21
  12.2 0.6 copy-start.9
  26.2 15.1 %collective-permute-start.1 = (bf16[128,2304]{1,0:T(8,128)(2,1)S(1)}, bf16[128,2304]{1,0:T(8,128)(2,1)}, u32[]{:S(2)}, u32[]{:S(2)}) collective-permute-start(bf16[128,2304]{1,0:T(8,128)(2,1)S(1)} %collective-permute-done), channel_id=1, source_target_pairs={{0,1},{1,2},{2,3},{3,0},{4,5},{5,6},{6,7},{7,4},{8,9},{9,10},{10,1... | collective-permute-start | bytes 1769480 | tf_op jit(solution)/shard_map/ppermute | solution.py:21
  41.3 14.4 %collective-permute-start.2 = (bf16[128,2304]{1,0:T(8,128)(2,1)}, bf16[128,2304]{1,0:T(8,128)(2,1)}, u32[]{:S(2)}, u32[]{:S(2)}) collective-permute-start(bf16[128,2304]{1,0:T(8,128)(2,1)} %collective-permute-done.1), channel_id=1, source_target_pairs={{0,1},{1,2},{2,3},{3,0},{4,5},{5,6},{6,7},{7,4},{8,9},{9,10},{10,1... | collective-permute-start | bytes 1769480 | tf_op jit(solution)/shard_map/ppermute | solution.py:21
  58.0 2.9 %copy-start.12 = (f32[2304]{0:T(1024)S(1)}, f32[2304]{0:T(1024)}, u32[]{:S(2)}) copy-start(f32[2304]{0:T(1024)} %param.17) | copy-start | bytes 27652
  60.4 4.9 %copy-start.4 = (bf16[1024,2304]{1,0:T(8,128)(2,1)}, bf16[1024,2304]{1,0:T(8,128)(2,1)S(1)}, u32[]{:S(2)}) copy-start(bf16[1024,2304]{1,0:T(8,128)(2,1)S(1)} %constant_dynamic-update-slice_fusion) | copy-start | bytes 14155780
  65.3 4.6 %copy-start.7 = (s32[512]{0:T(512)S(1)}, s32[512]{0:T(512)}, u32[]{:S(2)}) copy-start(s32[512]{0:T(512)} %param.23) | copy-start | bytes 6148
  65.3 4.7 %copy-start.10 = (s32[16]{0:T(128)S(1)}, s32[16]{0:T(128)}, u32[]{:S(2)}) copy-start(s32[16]{0:T(128)} %param.25) | copy-start | bytes 196
  65.3 30.7 %copy-start.11 = (s32[64]{0:T(128)S(1)}, s32[64]{0:T(128)}, u32[]{:S(2)}) copy-start(s32[64]{0:T(128)} %param.24) | copy-start | bytes 772
  65.3 40.0 %copy-start.13 = (f32[2304]{0:T(1024)S(1)}, f32[2304]{0:T(1024)}, u32[]{:S(2)}) copy-start(f32[2304]{0:T(1024)} %param.17) | copy-start | bytes 27652
  68.1 104.3 %all-gather.11.cloned.1.call-start = ((), (), s32[]{:S(2)}) async-start(), calls=%async_computation.3 | async-start | bytes 2359296 | tf_op jit(solution)/shard_map/all_gather | solution.py:190
  69.9 178.0 %reduce-scatter.2.cloned.1.call-start = ((), (), s32[]{:S(2)}) async-start(), calls=%async_computation.2 | async-start | bytes 5898240 | tf_op jit(solution)/shard_map/reduce_scatter | solution.py:200
  124.8 6.0 %copy-start.1 = (pred[512,1024]{0,1:T(8,128)(4,1)}, pred[512,1024]{0,1:T(8,128)(4,1)S(1)}, u32[]{:S(2)}) copy-start(pred[512,1024]{0,1:T(8,128)(4,1)S(1)} %and_and_fusion.5) | copy-start | bytes 1572868 | tf_op jit(solution)/shard_map/while
  136.8 6.0 %copy-start.1 = (pred[512,1024]{0,1:T(8,128)(4,1)}, pred[512,1024]{0,1:T(8,128)(4,1)S(1)}, u32[]{:S(2)}) copy-start(pred[512,1024]{0,1:T(8,128)(4,1)S(1)} %and_and_fusion.5) | copy-start | bytes 1572868 | tf_op jit(solution)/shard_map/while
  149.0 6.0 %copy-start.1 = (pred[512,1024]{0,1:T(8,128)(4,1)}, pred[512,1024]{0,1:T(8,128)(4,1)S(1)}, u32[]{:S(2)}) copy-start(pred[512,1024]{0,1:T(8,128)(4,1)S(1)} %and_and_fusion.5) | copy-start | bytes 1572868 | tf_op jit(solution)/shard_map/while
  161.2 6.0 %copy-start.1 = (pred[512,1024]{0,1:T(8,128)(4,1)}, pred[512,1024]{0,1:T(8,128)(4,1)S(1)}, u32[]{:S(2)}) copy-start(pred[512,1024]{0,1:T(8,128)(4,1)S(1)} %and_and_fusion.5) | copy-start | bytes 1572868 | tf_op jit(solution)/shard_map/while
  174.2 2.7 %copy-start.5 = (f32[512,2,256]{2,0,1:T(8,128)S(1)}, f32[512,2,256]{2,0,1:T(8,128)}, u32[]{:S(2)}) copy-start(f32[512,2,256]{2,0,1:T(8,128)} %get-tuple-element.684) | copy-start | bytes 3145732 | tf_op jit(solution)/shard_map/while
  178.8 1.0 copy-start.6
  181.6 2.7 %copy-start.5 = (f32[512,2,256]{2,0,1:T(8,128)S(1)}, f32[512,2,256]{2,0,1:T(8,128)}, u32[]{:S(2)}) copy-start(f32[512,2,256]{2,0,1:T(8,128)} %get-tuple-element.684) | copy-start | bytes 3145732 | tf_op jit(solution)/shard_map/while
  186.2 1.0 copy-start.6
  192.5 56.9 %copy-start.3 = (bf16[128,2304]{1,0:T(8,128)(2,1)S(1)}, bf16[128,2304]{1,0:T(8,128)(2,1)}, u32[]{:S(2)}) copy-start(bf16[128,2304]{1,0:T(8,128)(2,1)} %param.16) | copy-start | bytes 1769476
  192.5 56.9 %copy-start.8 = (f32[2304]{0:T(1024)S(1)}, f32[2304]{0:T(1024)}, u32[]{:S(2)}) copy-start(f32[2304]{0:T(1024)} %param.18) | copy-start | bytes 27652
Sparse Core Ops, SparseCore 0:
  68.3 45.7 all-gather.8
  115.6 28.0 all-gather.10
  192.6 55.2 reduce-scatter.1
